TPU v7x, 32 devices: a whole 2x2x4 slice. The times are simulated.
32 devices in a mesh: patch: 16 (over z, y, x), rep: 2 (over core).
Axes of the slice: x: 2, y: 2, z: 4, core: 2. Of those that a mesh axis runs over, the one named last changes fastest.
Arguments:
- tokens: bfloat16 [8192, 512], P(('patch', 'rep')), may hold values from -6 to 6
- cotangent: bfloat16 [8192, 512], P(('patch', 'rep')), may hold values from -6 to 6
- dest: int32 [8192], P(('patch', 'rep')), may hold values from 0 to 15, as said below
- neighbours: int32 [8192, 16], P(('patch', 'rep')), may hold values from 0 to 8191, as said below
- w_qkv: bfloat16 [512, 1536], replicated, may hold values from -0.25 to 0.25
- w_out: bfloat16 [512, 512], replicated, may hold values from -1 to 1
- w_up: bfloat16 [512, 2048], replicated, may hold values from -0.25 to 0.25
- w_down: bfloat16 [2048, 512], replicated, may hold values from -0.125 to 0.125
- ada_attn: float32 [32, 1024], replicated, may hold values from -0.5 to 0.5
- ada_mlp: float32 [32, 1024], replicated, may hold values from -0.5 to 0.5
- cond: float32 [32], replicated, may hold values from -4 to 4
Outputs:
- output: bfloat16 [8192, 512], P(('patch', 'rep'))
- grad_tokens: bfloat16 [8192, 512], P(('patch', 'rep'))
- grad_qkv: float32 [512, 1536], replicated
- grad_out: float32 [512, 512], replicated
- grad_up: float32 [512, 2048], replicated
- grad_down: float32 [2048, 512], replicated
- grad_ada_attn: float32 [32, 1024], replicated
- grad_ada_mlp: float32 [32, 1024], replicated
- grad_cond: float32 [32], replicated
Inputs may be any that keep to these rules, and one draw needn't show every extreme that they name: `dest`: within each index of rep, every patch receives exactly 256 rows; one device sends at most 17 rows to one patch, and each device sends exactly 17 rows to some patch. neighbours[i, 0] = i; every other neighbour of a node in patch q lies in the rows of the same index of rep in patch q - 1, q or q + 1, counted cyclically over 16 patches; positions may repeat.
All inputs are finite; a program needn't handle non-finite values.
Results may differ from a plain program's by a relative error of at most 0.013.
Values may be sent and summed in bfloat16 or wider, within the bound.
A program may use at most 128 MiB of HBM per device.

v0:
```python
import jax
import jax.numpy as jnp
from jax import lax
from jax.sharding import PartitionSpec as P

H = 4
HD = 128
NEIGH = 16
NORM_EPS = 1e-05


def extended(cells, sides, width):
    for axis, dim in sides:
        count = lax.axis_size(axis)
        head = lax.slice_in_dim(cells, 0, width, axis=dim)
        tail = lax.slice_in_dim(cells, cells.shape[dim] - width, cells.shape[dim], axis=dim)
        cells = jnp.concatenate(
            [
                lax.ppermute(tail, axis, [(i, (i + 1) % count) for i in range(count)]),
                cells,
                lax.ppermute(head, axis, [((i + 1) % count, i) for i in range(count)]),
            ],
            axis=dim,
        )
    return cells


def from_behind(array, axis, by):
    size = lax.axis_size(axis)
    return lax.ppermute(array, axis, [(i, (i + by) % size) for i in range(size)])


def norm_parts(values_in):
    centre = jnp.mean(values_in, axis=-1, keepdims=True)
    centred = values_in - centre
    inverse = lax.rsqrt(jnp.mean(centred * centred, axis=-1, keepdims=True) + NORM_EPS)
    return (centred * inverse, inverse)


def norm_back(grad_normed, plain, inverse, coeffs):
    feature_width = plain.shape[-1]
    scaled = grad_normed * (1.0 + coeffs[:feature_width])
    inner = (
        scaled
        - jnp.mean(scaled, axis=-1, keepdims=True)
        - plain * jnp.mean(scaled * plain, axis=-1, keepdims=True)
    )
    coeff_grad = jnp.concatenate(
        [jnp.sum(grad_normed * plain, axis=0), jnp.sum(grad_normed, axis=0)]
    )
    return (inverse * inner, coeff_grad)


def local(tokens, cotangent, dest, neighbours, w_qkv, w_out, w_up, w_down, ada_attn, ada_mlp, cond):
    highest = lax.Precision.HIGHEST
    row_count = tokens.shape[0]
    feature_width = tokens.shape[1]
    patch_count = lax.axis_size("patch")
    group_count = lax.axis_size("rep")
    capacity = row_count // patch_count + 1
    one_hot = (dest[:, None] == jnp.arange(patch_count, dtype=jnp.int32)[None, :]).astype(jnp.int32)
    earlier = jnp.cumsum(one_hot, axis=0) - one_hot
    slot_index = jnp.sum(earlier * one_hot, axis=1)
    sent_counts = jnp.sum(one_hot, axis=0)
    flat_slot = dest * capacity + slot_index
    outgoing = jnp.zeros((patch_count * capacity, 2 * feature_width), jnp.bfloat16)
    outgoing = outgoing.at[flat_slot].set(jnp.concatenate([tokens, cotangent], axis=1))
    arrived, arrived_counts = (
        lax.all_to_all(
            outgoing.reshape(patch_count, capacity, 2 * feature_width),
            "patch",
            split_axis=0,
            concat_axis=0,
            tiled=True,
        ),
        lax.all_to_all(sent_counts[:, None], "patch", split_axis=0, concat_axis=0, tiled=True),
    )
    counts_in = arrived_counts[:, 0]
    offsets = jnp.cumsum(counts_in) - counts_in
    columns = jnp.arange(capacity, dtype=jnp.int32)
    target = jnp.where(
        columns[None, :] < counts_in[:, None], offsets[:, None] + columns[None, :], row_count
    ).reshape(-1)
    placed = (
        jnp.zeros((row_count + 1, 2 * feature_width), jnp.bfloat16)
        .at[target]
        .set(arrived.reshape(-1, 2 * feature_width))[:row_count]
    )
    node_rows = placed[:, :feature_width].astype(jnp.float32)
    upstream = placed[:, feature_width:]
    coeff_attn = jnp.dot(cond, ada_attn, precision=highest)
    coeff_mlp = jnp.dot(cond, ada_mlp, precision=highest)
    plain_first, inv_first = norm_parts(node_rows)
    normed = (plain_first * (1.0 + coeff_attn[:feature_width]) + coeff_attn[feature_width:]).astype(
        jnp.bfloat16
    )
    projected = jnp.dot(normed, w_qkv, preferred_element_type=jnp.float32)
    queries = projected[:, :feature_width].astype(jnp.bfloat16)
    key_value = projected[:, feature_width:].astype(jnp.bfloat16)
    beside_all = extended(normed, (("patch", 0),), row_count)
    side_rows = jnp.concatenate([beside_all[:row_count], beside_all[2 * row_count :]], axis=0)
    side_kv = jnp.dot(
        side_rows, w_qkv[:, feature_width:], preferred_element_type=jnp.float32
    ).astype(jnp.bfloat16)
    kv_table = jnp.concatenate([side_kv[:row_count], key_value, side_kv[row_count:]], axis=0)
    my_patch = lax.axis_index("patch")
    owners = neighbours // row_count // group_count
    local_row = neighbours % row_count
    rel_patch = (owners - my_patch) % patch_count
    table_index = jnp.where(
        rel_patch == 0,
        row_count + local_row,
        jnp.where(rel_patch == 1, 2 * row_count + local_row, local_row),
    )
    block_rows = min(512, row_count)
    block_count = row_count // block_rows
    score_scale = 1.0 / HD**0.5

    def gather_block(index_block):
        gathered = kv_table[index_block]
        key_block = gathered[..., :feature_width].reshape(block_rows, NEIGH, H, HD)
        value_block = gathered[..., feature_width:].reshape(block_rows, NEIGH, H, HD)
        return (key_block, value_block)

    def forward_block(pieces):
        query_block, index_block = pieces
        key_block, value_block = gather_block(index_block)
        scores = (
            jnp.einsum(
                "bhd,bjhd->bhj",
                query_block.reshape(block_rows, H, HD),
                key_block,
                preferred_element_type=jnp.float32,
            )
            * score_scale
        )
        row_max = jnp.max(scores, axis=-1, keepdims=True)
        row_total = jnp.sum(jnp.exp(scores - row_max), axis=-1, keepdims=True)
        log_total = row_max + jnp.log(row_total)
        weights = jnp.exp(scores - log_total).astype(jnp.bfloat16)
        mixture = jnp.einsum(
            "bhj,bjhd->bhd", weights, value_block, preferred_element_type=jnp.float32
        )
        return (mixture.reshape(block_rows, feature_width).astype(jnp.bfloat16), log_total[..., 0])

    query_blocks = queries.reshape(block_count, block_rows, feature_width)
    index_blocks = table_index.reshape(block_count, block_rows, NEIGH)
    heads_out, log_totals = lax.map(forward_block, (query_blocks, index_blocks))
    heads_out = heads_out.reshape(row_count, feature_width)
    residual = node_rows + jnp.dot(heads_out, w_out, preferred_element_type=jnp.float32)
    plain_second, inv_second = norm_parts(residual)
    normed_mlp = (
        plain_second * (1.0 + coeff_mlp[:feature_width]) + coeff_mlp[feature_width:]
    ).astype(jnp.bfloat16)
    up_proj = jnp.dot(normed_mlp, w_up, preferred_element_type=jnp.float32)
    activation = jax.nn.silu(up_proj).astype(jnp.bfloat16)
    output_rows = residual + jnp.dot(activation, w_down, preferred_element_type=jnp.float32)
    gradient_down = jnp.einsum(
        "ri,rj->ij", activation, upstream, preferred_element_type=jnp.float32
    )
    grad_act = jnp.einsum("rj,ij->ri", upstream, w_down, preferred_element_type=jnp.float32)
    sigmoid_up = jax.nn.sigmoid(up_proj)
    grad_upproj = (grad_act * sigmoid_up * (1.0 + up_proj * (1.0 - sigmoid_up))).astype(
        jnp.bfloat16
    )
    gradient_up = jnp.einsum(
        "ri,rj->ij", normed_mlp, grad_upproj, preferred_element_type=jnp.float32
    )
    grad_normed_mlp = jnp.einsum("rj,ij->ri", grad_upproj, w_up, preferred_element_type=jnp.float32)
    grad_resid_norm, coeff_mlp_grad = norm_back(
        grad_normed_mlp, plain_second, inv_second, coeff_mlp
    )
    grad_residual = upstream.astype(jnp.float32) + grad_resid_norm
    grad_branch = grad_residual.astype(jnp.bfloat16)
    gradient_out = jnp.einsum(
        "ri,rj->ij", heads_out, grad_branch, preferred_element_type=jnp.float32
    )
    grad_heads = jnp.einsum(
        "rj,ij->ri", grad_branch, w_out, preferred_element_type=jnp.float32
    ).astype(jnp.bfloat16)

    def backward_block(table_grad, pieces):
        query_block, index_block, log_block, heads_grad = pieces
        key_block, value_block = gather_block(index_block)
        query_heads = query_block.reshape(block_rows, H, HD)
        scores = (
            jnp.einsum("bhd,bjhd->bhj", query_heads, key_block, preferred_element_type=jnp.float32)
            * score_scale
        )
        weights = jnp.exp(scores - log_block[..., None])
        weights_low = weights.astype(jnp.bfloat16)
        grad_heads_block = heads_grad.reshape(block_rows, H, HD)
        grad_weights = jnp.einsum(
            "bhd,bjhd->bhj", grad_heads_block, value_block, preferred_element_type=jnp.float32
        )
        grad_scores = weights * (
            grad_weights - jnp.sum(weights * grad_weights, axis=-1, keepdims=True)
        )
        scores_low = grad_scores.astype(jnp.bfloat16)
        grad_query = (
            jnp.einsum("bhj,bjhd->bhd", scores_low, key_block, preferred_element_type=jnp.float32)
            * score_scale
        )
        grad_key = (
            jnp.einsum("bhj,bhd->bjhd", scores_low, query_heads, preferred_element_type=jnp.float32)
            * score_scale
        )
        grad_value = jnp.einsum(
            "bhj,bhd->bjhd", weights_low, grad_heads_block, preferred_element_type=jnp.float32
        )
        pair_grad = jnp.concatenate(
            [
                grad_key.reshape(block_rows * NEIGH, feature_width),
                grad_value.reshape(block_rows * NEIGH, feature_width),
            ],
            axis=1,
        )
        table_grad = table_grad.at[index_block.reshape(-1)].add(pair_grad)
        return (table_grad, grad_query.reshape(block_rows, feature_width))

    table_grad, grad_queries = lax.scan(
        backward_block,
        jnp.zeros((3 * row_count, 2 * feature_width), jnp.float32),
        (
            query_blocks,
            index_blocks,
            log_totals,
            grad_heads.reshape(block_count, block_rows, feature_width),
        ),
    )
    returned = table_grad[row_count : 2 * row_count]
    for shift_by, side_piece in ((-1, table_grad[:row_count]), (1, table_grad[2 * row_count :])):
        returned = returned + from_behind(
            side_piece.astype(jnp.bfloat16), "patch", shift_by
        ).astype(side_piece.dtype)
    grad_projected = jnp.concatenate(
        [grad_queries.reshape(row_count, feature_width), returned], axis=1
    ).astype(jnp.bfloat16)
    gradient_proj = jnp.einsum(
        "ri,rj->ij", normed, grad_projected, preferred_element_type=jnp.float32
    )
    grad_normed = jnp.einsum("rj,ij->ri", grad_projected, w_qkv, preferred_element_type=jnp.float32)
    grad_input_norm, coeff_attn_grad = norm_back(grad_normed, plain_first, inv_first, coeff_attn)
    grad_input = (grad_residual + grad_input_norm).astype(jnp.bfloat16)
    gradient_proj, gradient_out, gradient_up, gradient_down, coeff_attn_grad, coeff_mlp_grad = (
        lax.psum(
            (
                gradient_proj,
                gradient_out,
                gradient_up,
                gradient_down,
                coeff_attn_grad,
                coeff_mlp_grad,
            ),
            ("patch", "rep"),
        )
    )
    gradient_ada_attn = jnp.outer(cond, coeff_attn_grad)
    gradient_ada_mlp = jnp.outer(cond, coeff_mlp_grad)
    gradient_cond = jnp.dot(ada_attn, coeff_attn_grad, precision=highest) + jnp.dot(
        ada_mlp, coeff_mlp_grad, precision=highest
    )
    leaving = jnp.concatenate([output_rows.astype(jnp.bfloat16), grad_input], axis=1)
    padded = jnp.concatenate([leaving, jnp.zeros((1, 2 * feature_width), jnp.bfloat16)], axis=0)
    going_back = padded[target].reshape(patch_count, capacity, 2 * feature_width)
    home_rows = lax.all_to_all(
        going_back, "patch", split_axis=0, concat_axis=0, tiled=True
    ).reshape(-1, 2 * feature_width)
    band_rows = home_rows[flat_slot]
    return (
        band_rows[:, :feature_width],
        band_rows[:, feature_width:],
        gradient_proj,
        gradient_out,
        gradient_up,
        gradient_down,
        gradient_ada_attn,
        gradient_ada_mlp,
        gradient_cond,
    )


def solution(mesh):
    return jax.shard_map(
        local,
        mesh=mesh,
        in_specs=(
            P(("patch", "rep"), None),
            P(("patch", "rep"), None),
            P(("patch", "rep")),
            P(("patch", "rep"), None),
            P(),
            P(),
            P(),
            P(),
            P(),
            P(),
            P(),
        ),
        out_specs=(
            P(("patch", "rep"), None),
            P(("patch", "rep"), None),
            P(),
            P(),
            P(),
            P(),
            P(),
            P(),
            P(),
        ),
        check_vma=False,
    )
```

profile of v0, /device:TPU:0, one launch (start us, length us, event | category | flops | bytes accessed | tf_op | source)
XLA Modules:
  0.0 489.2 jit_solution(324026931602704912)
XLA Ops:
  10.4 8.3 %all-to-all-start = ((s32[16,1,1]{2,1,0:T(1,128)}), s32[16,1,1]{2,1,0:T(1,128)S(1)}, u32[]{:S(2)}, u32[]{:S(2)}) async-start(s32[16,1,1]{2,1,0:T(1,128)} %copy.43), calls=%async_computation | async-start | bytes 16384 | tf_op jit(solution)/shard_map/all_to_all | solution.py:76
  26.0 5.3 %all-to-all-start.1 = ((bf16[16,17,1024]{2,1,0:T(8,128)(2,1)}), bf16[16,17,1024]{2,1,0:T(8,128)(2,1)S(1)}, u32[]{:S(2)}, u32[]{:S(2)}) async-start(bf16[16,17,1024]{2,1,0:T(8,128)(2,1)} %reshape.284), calls=%async_computation.1 | async-start | bytes 1572864 | tf_op jit(solution)/shard_map/all_to_all | solution.py:69
  32.7 17.8 %all-to-all-done.1 = bf16[16,17,1024]{2,1,0:T(8,128)(2,1)S(1)} async-done(((bf16[16,17,1024]{2,1,0:T(8,128)(2,1)}), bf16[16,17,1024]{2,1,0:T(8,128)(2,1)S(1)}, u32[]{:S(2)}, u32[]{:S(2)}) %all-to-all-start.1) | async-done | bytes 557088 | tf_op jit(solution)/shard_map/all_to_all | solution.py:69
  55.1 5.5 %collective-permute-start.1 = (bf16[256,512]{1,0:T(8,128)(2,1)S(1)}, bf16[256,512]{1,0:T(8,128)(2,1)}, u32[]{:S(2)}, u32[]{:S(2)}) collective-permute-start(bf16[256,512]{1,0:T(8,128)(2,1)S(1)} %fusion.38), channel_id=1, source_target_pairs={{2,0},{4,2},{6,4},{8,6},{10,8},{12,10},{14,12},{16,14},{18,16},{20... | collective-permute-start | bytes 786440 | tf_op jit(solution)/shard_map/ppermute | solution.py:21
  70.6 22.5 %gather_fusion = bf16[4096,1024]{1,0:T(8,128)(2,1)} fusion(bf16[768,1024]{1,0:T(8,128)(2,1)} %pad_maximum_fusion, s32[4096]{0:T(1024)S(1)} %broadcast_clamp_fusion), kind=kCustom, calls=%fused_computation | custom fusion | bytes 16793600 | tf_op jit(solution)/shard_map/while/body/eval_jaxpr/gather | solution.py:120
  93.1 5.9 %slice_bitcast_fusion = (bf16[256,2,4,8,128]{4,3,2,1,0:T(8,128)(2,1)}, bf16[256,2,4,8,128]{4,3,2,1,0:T(8,128)(2,1)S(1)}) fusion(bf16[256,16,1024]{2,1,0:T(8,128)(2,1)} %bitcast.129), kind=kLoop, calls=%fused_computation.22 | loop fusion | bytes 16777216
  105.5 3.5 fusion.7
  116.6 3.6 fusion.93
  126.9 4.4 fusion.9
  131.2 4.9 %multiply_multiply_fusion = f32[256,4,128,16]{2,1,3,0:T(4,128)S(1)} fusion(f32[256,4,16]{1,2,0:T(8,128)S(1)} %copy-done.2, f32[256,4,128]{2,1,0:T(4,128)S(1)} %copy-done.13), kind=kLoop, calls=%fused_computation.13 | loop fusion | flops 4194304 | bytes 8978432 | tf_op jit(solution)/shard_map/while/body/eval_jaxpr/mul | solution.py:205
  136.2 4.2 copy.98
  140.4 2.4 copy.49
  142.8 6.0 %broadcast_multiply_fusion = f32[256,4,128,16]{2,1,3,0:T(4,128)S(1)} fusion(f32[256,4,16]{1,2,0:T(8,128)} %copy.49, f32[256,4,128]{2,1,0:T(4,128)S(1)} %convert.31), kind=kLoop, calls=%fused_computation.24 | loop fusion | flops 2097152 | bytes 8978432 | tf_op jit(solution)/shard_map/while/body/eval_jaxpr/bhj,bhd->bjhd/dot_general | solution.py:208
  148.8 4.2 copy.97
  153.0 37.3 %scatter_custom_fusion.2 = f32[768,1024]{1,0:T(8,128)} fusion(s32[4096]{0:T(1024)} %bitcast.145, f32[4096,512]{1,0:T(8,128)} %bitcast.128, f32[]{:T(128)} %constant.147.clone.1, f32[4096,512]{1,0:T(8,128)} %bitcast.127, f32[]{:T(128)} %constant.132.clone.1), kind=kCustom, calls=%fused_computation.7 | custom fusion | flops 8388608 | bytes 19923968 | tf_op jit(solution)/shard_map/while/body/eval_jaxpr/scatter-add | solution.py:218
  192.5 3.5 collective-permute-start.2
  196.2 2.8 fusion.63
  199.1 8.3 %collective-permute-done.2 = bf16[256,1024]{1,0:T(8,128)(2,1)S(1)} collective-permute-done((bf16[256,1024]{1,0:T(8,128)(2,1)S(1)}, bf16[256,1024]{1,0:T(8,128)(2,1)S(1)}, u32[]{:S(2)}, u32[]{:S(2)}) %collective-permute-start.2) | collective-permute-done | bytes 524320 | tf_op jit(solution)/shard_map/ppermute | solution.py:30
  207.4 9.9 %collective-permute-done.3 = bf16[256,1024]{1,0:T(8,128)(2,1)S(1)} collective-permute-done((bf16[256,1024]{1,0:T(8,128)(2,1)S(1)}, bf16[256,1024]{1,0:T(8,128)(2,1)S(1)}, u32[]{:S(2)}, u32[]{:S(2)}) %collective-permute-start.3) | collective-permute-done | bytes 524320 | tf_op jit(solution)/shard_map/ppermute | solution.py:30
  221.7 3.1 fusion.20
  229.2 5.3 %all-to-all-start.2 = ((bf16[16,17,1024]{2,1,0:T(8,128)(2,1)}), bf16[16,17,1024]{2,1,0:T(8,128)(2,1)S(1)}, u32[]{:S(2)}, u32[]{:S(2)}) async-start(bf16[16,17,1024]{2,1,0:T(8,128)(2,1)} %reshape.294), calls=%async_computation.2 | async-start | bytes 1572864 | tf_op jit(solution)/shard_map/all_to_all | solution.py:266
  234.6 49.8 %all-reduce.1 = (f32[1024]{0:T(1024)S(1)}, f32[1024]{0:T(1024)S(1)}) all-reduce(f32[1024]{0:T(1024)S(1)} %pad_maximum_fusion.4, f32[1024]{0:T(1024)S(1)} %pad_maximum_fusion.5), channel_id=1, replica_groups=mesh['patch'=16,'rep'=2] {'patch','rep'}, use_global_device_ids=true, to_apply=%region_25.26 | all-reduce | flops 2048 | bytes 16384 | tf_op jit(solution)/shard_map/psum | solution.py:246
  288.4 182.0 %all-reduce.5.cloned.1.call-done = (f32[512,1536]{1,0:T(8,128)}, f32[512,512]{1,0:T(8,128)}, f32[512,2048]{1,0:T(8,128)}, f32[2048,512]{1,0:T(8,128)}) async-done(((f32[512,1536]{1,0:T(8,128)}, f32[512,512]{1,0:T(8,128)}, f32[512,2048]{1,0:T(8,128)}, f32[2048,512]{1,0:T(8,128)}), (f32[512,1536]{1,0:T(8,128)}, f32[512,512]{1,0:T(8,128)}, f32[512,2048]{1,0:T(8,128)}, ...) | async-done | bytes 12582928 | tf_op jit(solution)/shard_map/psum | solution.py:246
  470.4 3.9 copy.104
  (200 shorter events, 69.7 us)
Async XLA Ops:
  7.2 103.3 %copy-start = (bf16[512,2048]{1,0:T(8,128)(2,1)S(1)}, bf16[512,2048]{1,0:T(8,128)(2,1)}, u32[]{:S(2)}) copy-start(bf16[512,2048]{1,0:T(8,128)(2,1)} %param.17) | copy-start | bytes 6291460
  7.2 15.7 %copy-start.21 = (f32[32,1024]{1,0:T(8,128)S(1)}, f32[32,1024]{1,0:T(8,128)}, u32[]{:S(2)}) copy-start(f32[32,1024]{1,0:T(8,128)} %param.19) | copy-start | bytes 393220
  7.2 15.7 %copy-start.40 = (f32[32]{0:T(128)S(1)}, f32[32]{0:T(128)}, u32[]{:S(2)}) copy-start(f32[32]{0:T(128)} %param.21) | copy-start | bytes 388
  7.2 15.9 %copy-start.33 = (s32[256,16]{0,1:T(8,128)S(1)}, s32[256,16]{0,1:T(8,128)}, u32[]{:S(2)}) copy-start(s32[256,16]{0,1:T(8,128)} %param.14) | copy-start | bytes 49156
  7.2 16.1 %copy-start.23 = (f32[32,1024]{1,0:T(8,128)S(1)}, f32[32,1024]{1,0:T(8,128)}, u32[]{:S(2)}) copy-start(f32[32,1024]{1,0:T(8,128)} %param.20) | copy-start | bytes 393220
  10.4 15.5 %all-to-all-start = ((s32[16,1,1]{2,1,0:T(1,128)}), s32[16,1,1]{2,1,0:T(1,128)S(1)}, u32[]{:S(2)}, u32[]{:S(2)}) async-start(s32[16,1,1]{2,1,0:T(1,128)} %copy.43), calls=%async_computation | async-start | bytes 16384 | tf_op jit(solution)/shard_map/all_to_all | solution.py:76
  23.1 31.2 %copy-start.29 = (f32[512]{0:T(512)}, f32[512]{0:T(512)S(1)}, u32[]{:S(2)}) copy-start(f32[512]{0:T(512)S(1)} %get-tuple-element.81) | copy-start | bytes 6148
  26.0 24.5 %all-to-all-start.1 = ((bf16[16,17,1024]{2,1,0:T(8,128)(2,1)}), bf16[16,17,1024]{2,1,0:T(8,128)(2,1)S(1)}, u32[]{:S(2)}, u32[]{:S(2)}) async-start(bf16[16,17,1024]{2,1,0:T(8,128)(2,1)} %reshape.284), calls=%async_computation.1 | async-start | bytes 1572864 | tf_op jit(solution)/shard_map/all_to_all | solution.py:69
  31.3 439.1 %all-reduce.5.cloned.1.call-start = ((), (), s32[]{:S(2)}) async-start(), calls=%async_computation.3 | async-start | bytes 25165824 | tf_op jit(solution)/shard_map/psum | solution.py:246
  32.7 21.6 %copy-start.38 = (s32[272]{0:T(512)}, s32[272]{0:T(512)S(1)}, u32[]{:S(2)}) copy-start(s32[272]{0:T(512)S(1)} %fusion.84) | copy-start | bytes 3268
  54.5 10.9 %collective-permute-start = (bf16[256,512]{1,0:T(8,128)(2,1)S(1)}, bf16[256,512]{1,0:T(8,128)(2,1)}, u32[]{:S(2)}, u32[]{:S(2)}) collective-permute-start(bf16[256,512]{1,0:T(8,128)(2,1)S(1)} %fusion.38), channel_id=1, source_target_pairs={{0,2},{2,4},{4,6},{6,8},{8,10},{10,12},{12,14},{14,16},{16,18},{18... | collective-permute-start | bytes 786440 | tf_op jit(solution)/shard_map/ppermute | solution.py:19
  55.1 12.1 %collective-permute-start.1 = (bf16[256,512]{1,0:T(8,128)(2,1)S(1)}, bf16[256,512]{1,0:T(8,128)(2,1)}, u32[]{:S(2)}, u32[]{:S(2)}) collective-permute-start(bf16[256,512]{1,0:T(8,128)(2,1)S(1)} %fusion.38), channel_id=1, source_target_pairs={{2,0},{4,2},{6,4},{8,6},{10,8},{12,10},{14,12},{16,14},{18,16},{20... | collective-permute-start | bytes 786440 | tf_op jit(solution)/shard_map/ppermute | solution.py:21
  93.1 7.9 %copy-start.19 = (bf16[256,4,128,1]{2,3,1,0:T(2,128)(2,1)S(1)}, bf16[256,4,128,1]{2,3,1,0:T(2,128)(2,1)}, u32[]{:S(2)}) copy-start(bf16[256,4,128,1]{2,3,1,0:T(2,128)(2,1)} %reshape.365) | copy-start | bytes 786436
  116.6 5.0 %copy-start.6 = (bf16[256,2,4,8,128]{4,3,2,1,0:T(8,128)(2,1)S(1)}, bf16[256,2,4,8,128]{4,3,2,1,0:T(8,128)(2,1)}, u32[]{:S(2)}) copy-start(bf16[256,2,4,8,128]{4,3,2,1,0:T(8,128)(2,1)} %get-tuple-element.69) | copy-start | bytes 12582916
  190.2 5.8 %copy-start.18 = (f32[256,4,1,128]{3,2,1,0:T(1,128)S(1)}, f32[256,4,1,128]{3,2,1,0:T(1,128)}, u32[]{:S(2)}) copy-start(f32[256,4,1,128]{3,2,1,0:T(1,128)} %fusion.9) | copy-start | bytes 1572868
  192.5 14.9 %collective-permute-start.2 = (bf16[256,1024]{1,0:T(8,128)(2,1)S(1)}, bf16[256,1024]{1,0:T(8,128)(2,1)S(1)}, u32[]{:S(2)}, u32[]{:S(2)}) collective-permute-start(bf16[256,1024]{1,0:T(8,128)(2,1)S(1)} %get-tuple-element.71), channel_id=1, source_target_pairs={{0,30},{2,0},{4,2},{6,4},{8,6},{10,8},{12,10},{14,12},{16,14},{18,... | collective-permute-start | bytes 1572872 | tf_op jit(solution)/shard_map/ppermute | solution.py:30
  196.0 21.2 %collective-permute-start.3 = (bf16[256,1024]{1,0:T(8,128)(2,1)S(1)}, bf16[256,1024]{1,0:T(8,128)(2,1)S(1)}, u32[]{:S(2)}, u32[]{:S(2)}) collective-permute-start(bf16[256,1024]{1,0:T(8,128)(2,1)S(1)} %get-tuple-element.72), channel_id=1, source_target_pairs={{0,2},{2,4},{4,6},{6,8},{8,10},{10,12},{12,14},{14,16},{16,18},{18... | collective-permute-start | bytes 1572872 | tf_op jit(solution)/shard_map/ppermute | solution.py:30
  228.0 6.5 %copy-start.43 = (s32[256]{0:T(256)S(1)}, s32[256]{0:T(256)}, u32[]{:S(2)}) copy-start(s32[256]{0:T(256)} %copy-done.42) | copy-start | bytes 3076
  228.1 6.5 %copy-start.44 = (f32[512]{0:T(512)S(1)}, f32[512]{0:T(512)}, u32[]{:S(2)}) copy-start(f32[512]{0:T(512)} %get-tuple-element.45) | copy-start | bytes 6148
  228.1 6.5 %copy-start.45 = (f32[512]{0:T(512)S(1)}, f32[512]{0:T(512)}, u32[]{:S(2)}) copy-start(f32[512]{0:T(512)} %get-tuple-element.57) | copy-start | bytes 6148
  228.1 56.4 %copy-start.22 = (f32[32,1024]{1,0:T(8,128)S(1)}, f32[32,1024]{1,0:T(8,128)}, u32[]{:S(2)}) copy-start(f32[32,1024]{1,0:T(8,128)} %param.19) | copy-start | bytes 393220
  228.1 56.5 %copy-start.24 = (f32[32,1024]{1,0:T(8,128)S(1)}, f32[32,1024]{1,0:T(8,128)}, u32[]{:S(2)}) copy-start(f32[32,1024]{1,0:T(8,128)} %param.20) | copy-start | bytes 393220
  228.1 57.3 %copy-start.41 = (f32[32]{0:T(128)S(1)}, f32[32]{0:T(128)}, u32[]{:S(2)}) copy-start(f32[32]{0:T(128)} %param.21) | copy-start | bytes 388
  229.2 57.0 %all-to-all-start.2 = ((bf16[16,17,1024]{2,1,0:T(8,128)(2,1)}), bf16[16,17,1024]{2,1,0:T(8,128)(2,1)S(1)}, u32[]{:S(2)}, u32[]{:S(2)}) async-start(bf16[16,17,1024]{2,1,0:T(8,128)(2,1)} %reshape.294), calls=%async_computation.2 | async-start | bytes 1572864 | tf_op jit(solution)/shard_map/all_to_all | solution.py:266
  (32 other events, 87.3 us)
Sparse Core Ops, SparseCore 0:
  221.2 249.1 all-reduce.4
where the time goes:
time: 494 us; the launch traced here: 489 us
  waiting for transfers between devices  221 us (45%)
  local copies, waits for them, and re-layouts  74.2 us (15%)
  other arithmetic  64.3 us (13%)
  blocking collectives  49.8 us (10%)
  matrix products  35.6 us (7%)
  starting transfers between devices  28.7 us (6%)
  between operations  15.1 us (3%)
    psum x1, waiting for transfers between devices, local(): lax.psum((gradient_proj, gradient_out, gradient_up, gradient_down, coeff_...  182 us
    psum x1, blocking collectives, local(): lax.psum((gradient_proj, gradient_out, gradient_up, gradient_down, coeff_...  49.8 us
    scatter-add x1, other arithmetic, backward_block(): table_grad = table_grad.at[index_block.reshape(-1)].add(pair_grad)  37.3 us
    unnamed x102, local copies, waits for them, and re-layouts  31.4 us
    gather x1, local copies, waits for them, and re-layouts, gather_block(): gathered = kv_table[index_block]  22.5 us
    ppermute x2, waiting for transfers between devices, from_behind(): lax.ppermute(array, axis, [(i, (i + by) % size) for i in range(size)])  18.2 us
    all_to_all x1, waiting for transfers between devices, local(): lax.all_to_all(outgoing.reshape(patch_count, capacity, 2 * feature_width)...  17.8 us
  transfers between devices with their start and end apart: 8, of which 6 were waited for; matrix products, arithmetic and copies ran while one was open for 5% of the time, Pallas kernels for 0%

commit v1 on v0

--- a/solution.py
+++ b/solution.py
@@ -7,6 +7,28 @@
 HD = 128
 NEIGH = 16
 NORM_EPS = 1e-05
+
+
+def in_blocks(x, dim, peers):
+    before, after = (x.shape[:dim], x.shape[dim + 1 :])
+    return jnp.moveaxis(x.reshape(*before, peers, -1, *after), dim, 0)
+
+
+def joined_along(tiles, dim):
+    dims = list(tiles.shape[1:])
+    dims[dim] *= tiles.shape[0]
+    return jnp.moveaxis(tiles, 0, dim).reshape(dims)
+
+
+def pairwise_exchange(x, axis, split_dim, concat_dim):
+    size, here = (lax.axis_size(axis), lax.axis_index(axis))
+    blocks = in_blocks(x, split_dim, size)
+    outs = [blocks[here]]
+    for lap in range(1, size):
+        sent = blocks[here ^ lap]
+        outs.append(lax.ppermute(sent, axis, [(i, i ^ lap) for i in range(size)]))
+    blocks = jnp.stack(outs)[here ^ jnp.arange(size)]
+    return joined_along(blocks, concat_dim)
 
 
 def extended(cells, sides, width):
@@ -73,7 +95,7 @@
             concat_axis=0,
             tiled=True,
         ),
-        lax.all_to_all(sent_counts[:, None], "patch", split_axis=0, concat_axis=0, tiled=True),
+        pairwise_exchange(sent_counts[:, None], "patch", 0, 0),
     )
     counts_in = arrived_counts[:, 0]
     offsets = jnp.cumsum(counts_in) - counts_in

time: 494 us -> 511 us (1.034)
  starting transfers between devices: 28.7 us -> 50.3 us
  waiting for transfers between devices: 221 us -> 205 us
  local copies, waits for them, and re-layouts: 74.2 us -> 85.1 us
    ppermute x0 -> x15, starting transfers between devices: none -> 29.7 us  [pairwise_exchange(): outs.append(lax.ppermute(sent, axis, [(i, i ^ lap) for i in range(size)]))]
    all_to_all x1, waiting for transfers between devices: 17.8 us -> 0.01 us  [local(): lax.all_to_all(outgoing.reshape(patch_count, capacity, 2 * feature_width)...]
    another operation x4 -> x6, local copies, waits for them, and re-layouts: 4.77 us -> 14.9 us  [the longest x1 10.1 us: pairwise_exchange(): blocks = jnp.stack(outs)[here ^ jnp.arange(size)]]
    all_to_all x1 -> x0, starting transfers between devices: 8.31 us -> none  [local(): lax.all_to_all(sent_counts[:, None], 'patch', split_axis=0, concat_axis=0...]
    ppermute x0 -> x15, waiting for transfers between devices: none -> 7.08 us  [pairwise_exchange(): outs.append(lax.ppermute(sent, axis, [(i, i ^ lap) for i in range(size)]))]
  transfers between devices with their start and end apart: 8 -> 22, of which waited for: 6 -> 7; matrix products, arithmetic and copies ran while one was open for 5% -> 7% of each run, Pallas kernels for 0% -> 0%
where the time goes in v1:
time: 511 us; the launch traced here: 505 us
  waiting for transfers between devices  205 us (40%)
  local copies, waits for them, and re-layouts  85.1 us (17%)
  other arithmetic  63.9 us (13%)
  starting transfers between devices  50.3 us (10%)
  blocking collectives  49.6 us (10%)
  matrix products  35.7 us (7%)
  between operations  15.3 us (3%)
    psum x1, waiting for transfers between devices, local(): lax.psum((gradient_proj, gradient_out, gradient_up, gradient_down, coeff_...  182 us
    psum x1, blocking collectives, local(): lax.psum((gradient_proj, gradient_out, gradient_up, gradient_down, coeff_...  49.6 us
    scatter-add x1, other arithmetic, backward_block(): table_grad = table_grad.at[index_block.reshape(-1)].add(pair_grad)  37.3 us
    unnamed x102, local copies, waits for them, and re-layouts  31.5 us
    ppermute x15, starting transfers between devices, pairwise_exchange(): outs.append(lax.ppermute(sent, axis, [(i, i ^ lap) for i in range(size)]))  29.7 us
    gather x1, local copies, waits for them, and re-layouts, gather_block(): gathered = kv_table[index_block]  22.5 us
    ppermute x2, waiting for transfers between devices, from_behind(): lax.ppermute(array, axis, [(i, (i + by) % size) for i in range(size)])  15.1 us
  transfers between devices with their start and end apart: 22, of which 7 were waited for; matrix products, arithmetic and copies ran while one was open for 7% of the time, Pallas kernels for 0%

profile of v1, /device:TPU:0, one launch (start us, length us, event | category | flops | bytes accessed | tf_op | source)
XLA Modules:
  0.0 505.3 jit_solution(8094810165436750093)
XLA Ops:
  10.7 4.0 collective-permute-start.4
  25.5 4.9 all-to-all-start
  34.6 3.3 collective-permute-start.9
  37.9 3.7 collective-permute-start.11
  43.1 4.2 collective-permute-start.13
  58.7 10.1 %stack.63 = s32[16,1,1]{0,2,1:T(1,128)S(1)} concatenate(s32[1,1,1]{0,2,1:T(1,128)} %bitcast, s32[1,1,1]{0,2,1:T(1,128)} %bitcast.2, s32[1,1,1]{0,2,1:T(1,128)} %bitcast.4, s32[1,1,1]{0,2,1:T(1,128)} %bitcast.6, s32[1,1,1]{0,2,1:T(1,128)} %bitcast.8, s32[1,1,1]{0,2,1:T(1,128)} %bitcast.10, s32[1,1,1]{0,2,1:T(1,128)} %bitcast.12, s32[1,1,1]{0,2,1:T(1,128)} %bitcast.14, ...), dimensions={0} | concatenate | bytes 128 | tf_op jit(solution)/shard_map/stack | solution.py:30
  74.9 5.1 %collective-permute-start.16 = (bf16[256,512]{1,0:T(8,128)(2,1)S(1)}, bf16[256,512]{1,0:T(8,128)(2,1)}, u32[]{:S(2)}, u32[]{:S(2)}) collective-permute-start(bf16[256,512]{1,0:T(8,128)(2,1)S(1)} %fusion.38), channel_id=1, source_target_pairs={{2,0},{4,2},{6,4},{8,6},{10,8},{12,10},{14,12},{16,14},{18,16},{20... | collective-permute-start | bytes 786440 | tf_op jit(solution)/shard_map/ppermute | solution.py:43
  89.0 22.5 %gather_fusion.1 = bf16[4096,1024]{1,0:T(8,128)(2,1)} fusion(bf16[768,1024]{1,0:T(8,128)(2,1)} %pad_maximum_fusion, s32[4096]{0:T(1024)S(1)} %broadcast_clamp_fusion), kind=kCustom, calls=%fused_computation.1 | custom fusion | bytes 16793600 | tf_op jit(solution)/shard_map/while/body/eval_jaxpr/gather | solution.py:142
  111.5 5.9 %slice_bitcast_fusion = (bf16[256,2,4,8,128]{4,3,2,1,0:T(8,128)(2,1)}, bf16[256,2,4,8,128]{4,3,2,1,0:T(8,128)(2,1)S(1)}) fusion(bf16[256,16,1024]{2,1,0:T(8,128)(2,1)} %bitcast.163), kind=kLoop, calls=%fused_computation.23 | loop fusion | bytes 16777216
  123.9 3.5 fusion.7
  135.0 3.7 fusion.94
  145.2 4.4 fusion.9
  149.6 4.9 multiply_multiply_fusion
  154.5 4.2 copy.83
  161.2 6.0 %broadcast_multiply_fusion = f32[256,4,128,16]{2,1,3,0:T(4,128)S(1)} fusion(f32[256,4,16]{1,2,0:T(8,128)} %copy.34, f32[256,4,128]{2,1,0:T(4,128)S(1)} %convert.31), kind=kLoop, calls=%fused_computation.25 | loop fusion | flops 2097152 | bytes 8978432 | tf_op jit(solution)/shard_map/while/body/eval_jaxpr/bhj,bhd->bjhd/dot_general | solution.py:230
  167.2 4.2 copy.82
  171.4 37.3 %scatter_custom_fusion.2 = f32[768,1024]{1,0:T(8,128)} fusion(s32[4096]{0:T(1024)} %bitcast.178, f32[4096,512]{1,0:T(8,128)} %bitcast.162, f32[]{:T(128)} %constant.191.clone.1, f32[4096,512]{1,0:T(8,128)} %bitcast.161, f32[]{:T(128)} %constant.182.clone.1), kind=kCustom, calls=%fused_computation.8 | custom fusion | flops 8388608 | bytes 19923968 | tf_op jit(solution)/shard_map/while/body/eval_jaxpr/scatter-add | solution.py:240
  210.9 4.6 collective-permute-start.17
  218.5 7.3 %collective-permute-done.17 = bf16[256,1024]{1,0:T(8,128)(2,1)S(1)} collective-permute-done((bf16[256,1024]{1,0:T(8,128)(2,1)S(1)}, bf16[256,1024]{1,0:T(8,128)(2,1)S(1)}, u32[]{:S(2)}, u32[]{:S(2)}) %collective-permute-start.17) | collective-permute-done | bytes 524320 | tf_op jit(solution)/shard_map/ppermute | solution.py:52
  225.8 7.8 %collective-permute-done.18 = bf16[256,1024]{1,0:T(8,128)(2,1)S(1)} collective-permute-done((bf16[256,1024]{1,0:T(8,128)(2,1)S(1)}, bf16[256,1024]{1,0:T(8,128)(2,1)S(1)}, u32[]{:S(2)}, u32[]{:S(2)}) %collective-permute-start.18) | collective-permute-done | bytes 524320 | tf_op jit(solution)/shard_map/ppermute | solution.py:52
  245.5 4.9 all-to-all-start.1
  250.5 49.6 %all-reduce.1 = (f32[1024]{0:T(1024)S(1)}, f32[1024]{0:T(1024)S(1)}) all-reduce(f32[1024]{0:T(1024)S(1)} %pad_maximum_fusion.4, f32[1024]{0:T(1024)S(1)} %pad_maximum_fusion.5), channel_id=1, replica_groups=mesh['patch'=16,'rep'=2] {'patch','rep'}, use_global_device_ids=true, to_apply=%region_25.26 | all-reduce | flops 2048 | bytes 16384 | tf_op jit(solution)/shard_map/psum | solution.py:268
  304.1 182.5 %all-reduce.5.cloned.1.call-done = (f32[512,1536]{1,0:T(8,128)}, f32[512,512]{1,0:T(8,128)}, f32[512,2048]{1,0:T(8,128)}, f32[2048,512]{1,0:T(8,128)}) async-done(((f32[512,1536]{1,0:T(8,128)}, f32[512,512]{1,0:T(8,128)}, f32[512,2048]{1,0:T(8,128)}, f32[2048,512]{1,0:T(8,128)}), (f32[512,1536]{1,0:T(8,128)}, f32[512,512]{1,0:T(8,128)}, f32[512,2048]{1,0:T(8,128)}, ...) | async-done | bytes 12582928 | tf_op jit(solution)/shard_map/psum | solution.py:268
  486.5 3.9 copy.89
  (232 shorter events, 97.8 us)
Async XLA Ops:
  7.2 121.6 %copy-start = (bf16[512,2048]{1,0:T(8,128)(2,1)S(1)}, bf16[512,2048]{1,0:T(8,128)(2,1)}, u32[]{:S(2)}) copy-start(bf16[512,2048]{1,0:T(8,128)(2,1)} %param.17) | copy-start | bytes 6291460
  10.7 22.0 %collective-permute-start.4 = (s32[1,1]{1,0:T(1,128)}, s32[1,1]{1,0:T(1,128)}, u32[]{:S(2)}, u32[]{:S(2)}) collective-permute-start(s32[1,1]{1,0:T(1,128)} %bitcast.9), channel_id=1, source_target_pairs={{0,10},{2,8},{4,14},{6,12},{8,2},{10,0},{12,6},{14,4},{16,26},{18,... | collective-permute-start | bytes 20 | tf_op jit(solution)/shard_map/ppermute | solution.py:29
  14.6 19.9 %collective-permute-start.5 = (s32[1,1]{1,0:T(1,128)}, s32[1,1]{1,0:T(1,128)}, u32[]{:S(2)}, u32[]{:S(2)}) collective-permute-start(s32[1,1]{1,0:T(1,128)} %bitcast.11), channel_id=1, source_target_pairs={{0,12},{2,14},{4,8},{6,10},{8,4},{10,6},{12,0},{14,2},{16,28},{18,... | collective-permute-start | bytes 20 | tf_op jit(solution)/shard_map/ppermute | solution.py:29
  16.1 21.8 %collective-permute-start.6 = (s32[1,1]{1,0:T(1,128)}, s32[1,1]{1,0:T(1,128)}, u32[]{:S(2)}, u32[]{:S(2)}) collective-permute-start(s32[1,1]{1,0:T(1,128)} %bitcast.13), channel_id=1, source_target_pairs={{0,14},{2,12},{4,10},{6,8},{8,6},{10,4},{12,2},{14,0},{16,30},{18,... | collective-permute-start | bytes 20 | tf_op jit(solution)/shard_map/ppermute | solution.py:29
  17.5 20.4 %collective-permute-start.7 = (s32[1,1]{1,0:T(1,128)}, s32[1,1]{1,0:T(1,128)}, u32[]{:S(2)}, u32[]{:S(2)}) collective-permute-start(s32[1,1]{1,0:T(1,128)} %bitcast.15), channel_id=1, source_target_pairs={{0,16},{2,18},{4,20},{6,22},{8,24},{10,26},{12,28},{14,30},{16,0},... | collective-permute-start | bytes 20 | tf_op jit(solution)/shard_map/ppermute | solution.py:29
  20.1 21.5 %collective-permute-start.8 = (s32[1,1]{1,0:T(1,128)}, s32[1,1]{1,0:T(1,128)}, u32[]{:S(2)}, u32[]{:S(2)}) collective-permute-start(s32[1,1]{1,0:T(1,128)} %bitcast.17), channel_id=1, source_target_pairs={{0,18},{2,16},{4,22},{6,20},{8,26},{10,24},{12,30},{14,28},{16,2},... | collective-permute-start | bytes 20 | tf_op jit(solution)/shard_map/ppermute | solution.py:29
  25.5 44.5 %all-to-all-start = ((bf16[16,17,1024]{2,1,0:T(8,128)(2,1)}), bf16[16,17,1024]{2,1,0:T(8,128)(2,1)S(1)}, u32[]{:S(2)}, u32[]{:S(2)}) async-start(bf16[16,17,1024]{2,1,0:T(8,128)(2,1)} %reshape.329), calls=%async_computation | async-start | bytes 1572864 | tf_op jit(solution)/shard_map/all_to_all | solution.py:91
  30.4 456.1 %all-reduce.5.cloned.1.call-start = ((), (), s32[]{:S(2)}) async-start(), calls=%async_computation.2 | async-start | bytes 25165824 | tf_op jit(solution)/shard_map/psum | solution.py:268
  32.6 10.5 %collective-permute-start = (s32[1,1]{1,0:T(1,128)}, s32[1,1]{1,0:T(1,128)}, u32[]{:S(2)}, u32[]{:S(2)}) collective-permute-start(s32[1,1]{1,0:T(1,128)} %bitcast.1), channel_id=1, source_target_pairs={{0,2},{2,0},{4,6},{6,4},{8,10},{10,8},{12,14},{14,12},{16,18},{18,... | collective-permute-start | bytes 20 | tf_op jit(solution)/shard_map/ppermute | solution.py:29
  34.6 15.6 %collective-permute-start.9 = (s32[1,1]{1,0:T(1,128)}, s32[1,1]{1,0:T(1,128)}, u32[]{:S(2)}, u32[]{:S(2)}) collective-permute-start(s32[1,1]{1,0:T(1,128)} %bitcast.19), channel_id=1, source_target_pairs={{0,20},{2,22},{4,16},{6,18},{8,28},{10,30},{12,24},{14,26},{16,4},... | collective-permute-start | bytes 20 | tf_op jit(solution)/shard_map/ppermute | solution.py:29
  37.8 14.6 %collective-permute-start.10 = (s32[1,1]{1,0:T(1,128)}, s32[1,1]{1,0:T(1,128)}, u32[]{:S(2)}, u32[]{:S(2)}) collective-permute-start(s32[1,1]{1,0:T(1,128)} %bitcast.21), channel_id=1, source_target_pairs={{0,22},{2,20},{4,18},{6,16},{8,30},{10,28},{12,26},{14,24},{16,6},... | collective-permute-start | bytes 20 | tf_op jit(solution)/shard_map/ppermute | solution.py:29
  37.9 16.0 %collective-permute-start.11 = (s32[1,1]{1,0:T(1,128)}, s32[1,1]{1,0:T(1,128)}, u32[]{:S(2)}, u32[]{:S(2)}) collective-permute-start(s32[1,1]{1,0:T(1,128)} %bitcast.23), channel_id=1, source_target_pairs={{0,24},{2,26},{4,28},{6,30},{8,16},{10,18},{12,20},{14,22},{16,8},... | collective-permute-start | bytes 20 | tf_op jit(solution)/shard_map/ppermute | solution.py:29
  41.7 12.8 %collective-permute-start.12 = (s32[1,1]{1,0:T(1,128)}, s32[1,1]{1,0:T(1,128)}, u32[]{:S(2)}, u32[]{:S(2)}) collective-permute-start(s32[1,1]{1,0:T(1,128)} %bitcast.25), channel_id=1, source_target_pairs={{0,26},{2,24},{4,30},{6,28},{8,18},{10,16},{12,22},{14,20},{16,10}... | collective-permute-start | bytes 20 | tf_op jit(solution)/shard_map/ppermute | solution.py:29
  43.1 11.3 %collective-permute-start.13 = (s32[1,1]{1,0:T(1,128)}, s32[1,1]{1,0:T(1,128)}, u32[]{:S(2)}, u32[]{:S(2)}) collective-permute-start(s32[1,1]{1,0:T(1,128)} %bitcast.27), channel_id=1, source_target_pairs={{0,28},{2,30},{4,24},{6,26},{8,20},{10,22},{12,16},{14,18},{16,12}... | collective-permute-start | bytes 20 | tf_op jit(solution)/shard_map/ppermute | solution.py:29
  50.1 7.2 %collective-permute-start.14 = (s32[1,1]{1,0:T(1,128)}, s32[1,1]{1,0:T(1,128)}, u32[]{:S(2)}, u32[]{:S(2)}) collective-permute-start(s32[1,1]{1,0:T(1,128)} %bitcast.29), channel_id=1, source_target_pairs={{0,30},{2,28},{4,26},{6,24},{8,22},{10,20},{12,18},{14,16},{16,14}... | collective-permute-start | bytes 20 | tf_op jit(solution)/shard_map/ppermute | solution.py:29
  52.4 4.9 collective-permute-start.1
  53.9 4.8 collective-permute-start.2
  54.5 4.2 collective-permute-start.3
  73.9 10.9 %collective-permute-start.15 = (bf16[256,512]{1,0:T(8,128)(2,1)S(1)}, bf16[256,512]{1,0:T(8,128)(2,1)}, u32[]{:S(2)}, u32[]{:S(2)}) collective-permute-start(bf16[256,512]{1,0:T(8,128)(2,1)S(1)} %fusion.38), channel_id=1, source_target_pairs={{0,2},{2,4},{4,6},{6,8},{8,10},{10,12},{12,14},{14,16},{16,18},{18... | collective-permute-start | bytes 786440 | tf_op jit(solution)/shard_map/ppermute | solution.py:41
  74.9 10.7 %collective-permute-start.16 = (bf16[256,512]{1,0:T(8,128)(2,1)S(1)}, bf16[256,512]{1,0:T(8,128)(2,1)}, u32[]{:S(2)}, u32[]{:S(2)}) collective-permute-start(bf16[256,512]{1,0:T(8,128)(2,1)S(1)} %fusion.38), channel_id=1, source_target_pairs={{2,0},{4,2},{6,4},{8,6},{10,8},{12,10},{14,12},{16,14},{18,16},{20... | collective-permute-start | bytes 786440 | tf_op jit(solution)/shard_map/ppermute | solution.py:43
  210.9 14.9 %collective-permute-start.17 = (bf16[256,1024]{1,0:T(8,128)(2,1)S(1)}, bf16[256,1024]{1,0:T(8,128)(2,1)S(1)}, u32[]{:S(2)}, u32[]{:S(2)}) collective-permute-start(bf16[256,1024]{1,0:T(8,128)(2,1)S(1)} %get-tuple-element.71), channel_id=1, source_target_pairs={{0,30},{2,0},{4,2},{6,4},{8,6},{10,8},{12,10},{14,12},{16,14},{18,... | collective-permute-start | bytes 1572872 | tf_op jit(solution)/shard_map/ppermute | solution.py:52
  215.5 18.1 %collective-permute-start.18 = (bf16[256,1024]{1,0:T(8,128)(2,1)S(1)}, bf16[256,1024]{1,0:T(8,128)(2,1)S(1)}, u32[]{:S(2)}, u32[]{:S(2)}) collective-permute-start(bf16[256,1024]{1,0:T(8,128)(2,1)S(1)} %get-tuple-element.72), channel_id=1, source_target_pairs={{0,2},{2,4},{4,6},{6,8},{8,10},{10,12},{12,14},{14,16},{16,18},{18... | collective-permute-start | bytes 1572872 | tf_op jit(solution)/shard_map/ppermute | solution.py:52
  244.4 56.6 %copy-start.41 = (f32[32]{0:T(128)S(1)}, f32[32]{0:T(128)}, u32[]{:S(2)}) copy-start(f32[32]{0:T(128)} %param.21) | copy-start | bytes 388
  245.5 56.3 %all-to-all-start.1 = ((bf16[16,17,1024]{2,1,0:T(8,128)(2,1)}), bf16[16,17,1024]{2,1,0:T(8,128)(2,1)S(1)}, u32[]{:S(2)}, u32[]{:S(2)}) async-start(bf16[16,17,1024]{2,1,0:T(8,128)(2,1)} %reshape.339), calls=%async_computation.1 | async-start | bytes 1572864 | tf_op jit(solution)/shard_map/all_to_all | solution.py:288
  (46 other events, 375.3 us)
Sparse Core Ops, SparseCore 0:
  237.5 248.9 all-reduce.4
